TPU v7x, 32 devices: a whole 2x2x4 slice. The times are simulated.
32 devices in a mesh: dp: 16 (over z, y, core), seq: 2 (over x).
Axes of the slice: x: 2, y: 2, z: 4, core: 2. Of those that a mesh axis runs over, the one named last changes fastest.
Arguments:
- latents: float32 [16, 256, 1152], P('dp', 'seq'), may hold values from -6 to 6
- condition: float32 [8, 1152], replicated, may hold values from -6 to 6
- slot_latent: int32 [16, 1], P('dp'), may hold values from 0 to 7, as said below
- slot_counts: int32 [16], P('dp'), may hold values from 0 to 1, as said below
- output_gradient: float32 [16, 256, 1152], P('dp', 'seq'), may hold values from -6 to 6
- ada_weight: float32 [1152, 6912], P(None, ('dp', 'seq')), may hold values from -0.1875 to 0.1875
- ada_bias: float32 [6912], P(('dp', 'seq')), may hold values from -1.75 to 1.75
- qkv_weight: float32 [1152, 3456], P('dp', 'seq'), may hold values from -5 to 5, as said below
- qkv_bias: float32 [3456], P('seq'), may hold values from -1.25 to 1.25
- out_weight: float32 [1152, 1152], P('dp', 'seq'), may hold values from -0.75 to 0.75
- out_bias: float32 [1152], P('seq'), may hold values from -1.25 to 1.25
- up_weight: float32 [1152, 4608], P('dp', 'seq'), may hold values from -0.1875 to 0.1875
- up_bias: float32 [4608], P('seq'), may hold values from -1.25 to 1.25
- down_weight: float32 [4608, 1152], P('dp', 'seq'), may hold values from -0.09375 to 0.09375
- down_bias: float32 [1152], P('seq'), may hold values from -1.25 to 1.25
- mean_adaw: float32 [1152, 6912], P(None, ('dp', 'seq')), may hold values from -16 to 16
- mean_adab: float32 [6912], P(('dp', 'seq')), may hold values from -16 to 16
- mean_qkvw: float32 [1152, 3456], P('dp', 'seq'), may hold values from -16 to 16
- mean_qkvb: float32 [3456], P('seq'), may hold values from -16 to 16
- mean_outw: float32 [1152, 1152], P('dp', 'seq'), may hold values from -16 to 16
- mean_outb: float32 [1152], P('seq'), may hold values from -16 to 16
- mean_upw: float32 [1152, 4608], P('dp', 'seq'), may hold values from -16 to 16
- mean_upb: float32 [4608], P('seq'), may hold values from -16 to 16
- mean_downw: float32 [4608, 1152], P('dp', 'seq'), may hold values from -16 to 16
- mean_downb: float32 [1152], P('seq'), may hold values from -16 to 16
- sqmean_adaw: float32 [1152, 6912], P(None, ('dp', 'seq')), may hold values from 0.3 to 3
- sqmean_adab: float32 [6912], P(('dp', 'seq')), may hold values from 0.3 to 3
- sqmean_qkvw: float32 [1152, 3456], P('dp', 'seq'), may hold values from 0.3 to 3
- sqmean_qkvb: float32 [3456], P('seq'), may hold values from 0.3 to 3
- sqmean_outw: float32 [1152, 1152], P('dp', 'seq'), may hold values from 0.3 to 3
- sqmean_outb: float32 [1152], P('seq'), may hold values from 0.3 to 3
- sqmean_upw: float32 [1152, 4608], P('dp', 'seq'), may hold values from 0.3 to 3
- sqmean_upb: float32 [4608], P('seq'), may hold values from 0.3 to 3
- sqmean_downw: float32 [4608, 1152], P('dp', 'seq'), may hold values from 0.3 to 3
- sqmean_downb: float32 [1152], P('seq'), may hold values from 0.3 to 3
Outputs:
- block_output: float32 [16, 256, 1152], P('dp', 'seq')
- latent_gradient: float32 [16, 256, 1152], P('dp', 'seq')
- condition_grad: float32 [8, 1152], replicated
- grad_adaw: float32 [1152, 6912], P(None, ('dp', 'seq'))
- grad_adab: float32 [6912], P(('dp', 'seq'))
- grad_qkvw: float32 [1152, 3456], P('dp', 'seq')
- grad_qkvb: float32 [3456], P('seq')
- grad_outw: float32 [1152, 1152], P('dp', 'seq')
- grad_outb: float32 [1152], P('seq')
- grad_upw: float32 [1152, 4608], P('dp', 'seq')
- grad_upb: float32 [4608], P('seq')
- grad_downw: float32 [4608, 1152], P('dp', 'seq')
- grad_downb: float32 [1152], P('seq')
- newval_adaw: float32 [1152, 6912], P(None, ('dp', 'seq'))
- newval_adab: float32 [6912], P(('dp', 'seq'))
- newval_qkvw: float32 [1152, 3456], P('dp', 'seq')
- newval_qkvb: float32 [3456], P('seq')
- newval_outw: float32 [1152, 1152], P('dp', 'seq')
- newval_outb: float32 [1152], P('seq')
- newval_upw: float32 [1152, 4608], P('dp', 'seq')
- newval_upb: float32 [4608], P('seq')
- newval_downw: float32 [4608, 1152], P('dp', 'seq')
- newval_downb: float32 [1152], P('seq')
- newmean_adaw: float32 [1152, 6912], P(None, ('dp', 'seq'))
- newmean_adab: float32 [6912], P(('dp', 'seq'))
- newmean_qkvw: float32 [1152, 3456], P('dp', 'seq')
- newmean_qkvb: float32 [3456], P('seq')
- newmean_outw: float32 [1152, 1152], P('dp', 'seq')
- newmean_outb: float32 [1152], P('seq')
- newmean_upw: float32 [1152, 4608], P('dp', 'seq')
- newmean_upb: float32 [4608], P('seq')
- newmean_downw: float32 [4608, 1152], P('dp', 'seq')
- newmean_downb: float32 [1152], P('seq')
- newsqr_adaw: float32 [1152, 6912], P(None, ('dp', 'seq'))
- newsqr_adab: float32 [6912], P(('dp', 'seq'))
- newsqr_qkvw: float32 [1152, 3456], P('dp', 'seq')
- newsqr_qkvb: float32 [3456], P('seq')
- newsqr_outw: float32 [1152, 1152], P('dp', 'seq')
- newsqr_outb: float32 [1152], P('seq')
- newsqr_upw: float32 [1152, 4608], P('dp', 'seq')
- newsqr_upb: float32 [4608], P('seq')
- newsqr_downw: float32 [4608, 1152], P('dp', 'seq')
- newsqr_downb: float32 [1152], P('seq')
Inputs may be any that keep to these rules, and one draw needn't show every extreme that they name: `slot_counts`: live slots of a group come first; the entries sum to 8; some group has all 1 slots live in every draw, some groups may have none. `slot_latent`: the live slots name every latent exactly once; entries of slots that are not live are arbitrary latents. `qkv_weight`: query and value columns have entries of order 1152^-1/2; key columns may have entries up to the ends of the range.
All inputs are finite; a program needn't handle non-finite values.
Results may differ from a plain program's by a relative error of at most 0.012.
The roundings to bfloat16 on the way count: a program that leaves them out, or rounds other values in their place, can miss the bound.
Values may be sent and summed in bfloat16 or wider, within the bound.
A program may use at most 192 MiB of HBM per device.

v0:
```python
import jax
import jax.numpy as jnp
from jax import lax
from jax.sharding import PartitionSpec as P

H = 16
HD = 72
STEP = 2


EPS_NORM = 1e-06
GELU_COEF = 0.7978845608
GELU_CUBE = 0.044715
BETA_ONE = 0.9
BETA_TWO = 0.999
LEARN_RATE = 0.05
EPS_ADAM = 1e-08


def rounded(values):
    return lax.optimization_barrier(values.astype(jnp.bfloat16)).astype(jnp.float32)


def normalize(values):
    center = values - jnp.mean(values, axis=-1, keepdims=True)
    spread = lax.rsqrt(jnp.mean(center * center, axis=-1, keepdims=True) + EPS_NORM)
    return (center * spread, spread)


def norm_back(upstream, normed, spread):
    return spread * (
        upstream
        - jnp.mean(upstream, axis=-1, keepdims=True)
        - normed * jnp.mean(upstream * normed, axis=-1, keepdims=True)
    )


def gelu_tanh(values):
    tanh_part = jnp.tanh(GELU_COEF * (values + GELU_CUBE * values * values * values))
    return 0.5 * values * (1.0 + tanh_part)


def gelu_slope(values):
    tanh_part = jnp.tanh(GELU_COEF * (values + GELU_CUBE * values * values * values))
    return 0.5 * (1.0 + tanh_part) + 0.5 * values * (1.0 - tanh_part * tanh_part) * GELU_COEF * (
        1.0 + 3.0 * GELU_CUBE * values * values
    )


def silu_slope(values):
    sigmoid_part = jax.nn.sigmoid(values)
    return sigmoid_part * (1.0 + values * (1.0 - sigmoid_part))


def adamw_step(parameter, gradient, first_mom, second):
    first_new = BETA_ONE * first_mom + (1.0 - BETA_ONE) * gradient
    second_new = BETA_TWO * second + (1.0 - BETA_TWO) * gradient * gradient
    first_hat = first_new / (1.0 - BETA_ONE**STEP)
    second_hat = second_new / (1.0 - BETA_TWO**STEP)
    return (
        parameter - LEARN_RATE * first_hat / (jnp.sqrt(second_hat) + EPS_ADAM),
        first_new,
        second_new,
    )


def collect(weight, bias):
    pieces, bias_full = (
        lax.all_gather(weight.astype(jnp.bfloat16), "seq", axis=1, tiled=True),
        lax.all_gather(bias.astype(jnp.bfloat16), "seq", axis=0, tiled=True),
    )
    return (lax.all_gather(pieces, "dp", axis=0, tiled=True), bias_full.astype(jnp.float32))


def collect_again(weight):
    pieces = lax.all_gather(weight.astype(jnp.bfloat16), "seq", axis=1, tiled=True)
    return lax.all_gather(pieces, "dp", axis=0, tiled=True)


def spread_grad(left, right):
    term = jnp.einsum("rc,rd->cd", left, right, preferred_element_type=jnp.float32)
    partial_value = lax.psum_scatter(term, "dp", scatter_dimension=0, tiled=True)
    return lax.psum_scatter(partial_value, "seq", scatter_dimension=1, tiled=True)


def on_device(
    latents,
    condition,
    slot_latent,
    slot_counts,
    output_gradient,
    ada_weight,
    ada_bias,
    qkv_weight,
    qkv_bias,
    out_weight,
    out_bias,
    up_weight,
    up_bias,
    down_weight,
    down_bias,
    mean_adaw,
    mean_adab,
    mean_qkvw,
    mean_qkvb,
    mean_outw,
    mean_outb,
    mean_upw,
    mean_upb,
    mean_downw,
    mean_downb,
    sqmean_adaw,
    sqmean_adab,
    sqmean_qkvw,
    sqmean_qkvb,
    sqmean_outw,
    sqmean_outb,
    sqmean_upw,
    sqmean_upb,
    sqmean_downw,
    sqmean_downb,
):
    slot_total, tok_dev, model_width = latents.shape
    row_count = slot_total * tok_dev
    scale = HD ** (-0.5)
    live_slots = jnp.arange(slot_total) < slot_counts[0]
    live_mask = live_slots[:, None, None]
    latent_count = condition.shape[0]
    slot_matches = (
        (slot_latent[0][:, None] == jnp.arange(latent_count)[None, :]) & live_slots[:, None]
    ).astype(jnp.float32)
    silu_cond = jax.nn.silu(condition).astype(jnp.bfloat16)
    mod_cols = jnp.dot(
        silu_cond, ada_weight.astype(jnp.bfloat16), preferred_element_type=jnp.float32
    ) + rounded(ada_bias)
    modulation = lax.all_gather(mod_cols, ("dp", "seq"), axis=1, tiled=True)
    slot_mod = jnp.dot(slot_matches, modulation, precision=lax.Precision.HIGHEST)[:, None, :]
    shift_att, scale_att, gate_att, shift_mlp, scale_mlp, gate_mlp = jnp.split(slot_mod, 6, axis=2)
    upstream = jnp.where(live_mask, output_gradient, 0.0)
    mat_qkv, vec_qkv = collect(qkv_weight, qkv_bias)
    normed_att, spread_att = normalize(latents)
    attn_in = (
        (normed_att * (1.0 + scale_att) + shift_att)
        .astype(jnp.bfloat16)
        .reshape(row_count, model_width)
    )
    qkv_all = (jnp.dot(attn_in, mat_qkv, preferred_element_type=jnp.float32) + vec_qkv).astype(
        jnp.bfloat16
    )
    queries = qkv_all[:, :model_width].reshape(slot_total, tok_dev, H, HD)
    keys_own = qkv_all[:, model_width : 2 * model_width].reshape(slot_total, tok_dev, model_width)
    values_own = qkv_all[:, 2 * model_width :].reshape(slot_total, tok_dev, model_width)
    keys_all, values_all = (
        lax.all_gather(keys_own, "seq", axis=1, tiled=True),
        lax.all_gather(values_own, "seq", axis=1, tiled=True),
    )
    keys_heads = keys_all.reshape(slot_total, -1, H, HD)
    values_heads = values_all.reshape(slot_total, -1, H, HD)
    scores = (
        jnp.einsum("sqhd,skhd->shqk", queries, keys_heads, preferred_element_type=jnp.float32)
        * scale
    )
    row_max = jnp.max(scores, axis=-1, keepdims=True)
    row_total = jnp.sum(jnp.exp(scores - row_max), axis=-1, keepdims=True)
    attn_probs = jnp.exp(scores - row_max) / row_total
    probs_b = attn_probs.astype(jnp.bfloat16)
    attended = jnp.einsum(
        "shqk,skhd->sqhd", probs_b, values_heads, preferred_element_type=jnp.float32
    )
    attended_b = attended.reshape(row_count, model_width).astype(jnp.bfloat16)
    mat_out, vec_out = collect(out_weight, out_bias)
    branch_att = (
        jnp.dot(attended_b, mat_out, preferred_element_type=jnp.float32) + vec_out
    ).reshape(slot_total, tok_dev, model_width)
    middle = latents + gate_att * branch_att
    normed_mlp, spread_mlp = normalize(middle)
    mlp_in = (
        (normed_mlp * (1.0 + scale_mlp) + shift_mlp)
        .astype(jnp.bfloat16)
        .reshape(row_count, model_width)
    )
    mat_up, vec_up = collect(up_weight, up_bias)
    hidden = jnp.dot(mlp_in, mat_up, preferred_element_type=jnp.float32) + vec_up
    activated = gelu_tanh(hidden).astype(jnp.bfloat16)
    mat_down, vec_down = collect(down_weight, down_bias)
    branch_mlp = (
        jnp.dot(activated, mat_down, preferred_element_type=jnp.float32) + vec_down
    ).reshape(slot_total, tok_dev, model_width)
    block_output = jnp.where(live_mask, middle + gate_mlp * branch_mlp, 0.0)
    mat_down = collect_again(down_weight)
    back_down = upstream * gate_mlp
    back_down_b = back_down.astype(jnp.bfloat16).reshape(row_count, model_width)
    grad_downw = spread_grad(activated, back_down_b)
    sum_downb = jnp.sum(back_down, axis=(0, 1))
    back_hidden = jnp.einsum(
        "rd,fd->rf", back_down_b, mat_down, preferred_element_type=jnp.float32
    ) * gelu_slope(hidden)
    back_hidden_b = back_hidden.astype(jnp.bfloat16)
    mat_up = collect_again(up_weight)
    grad_upw = spread_grad(mlp_in, back_hidden_b)
    sum_upb = jnp.sum(back_hidden, axis=0)
    back_mlp_in = jnp.einsum(
        "rf,cf->rc", back_hidden_b, mat_up, preferred_element_type=jnp.float32
    ).reshape(slot_total, tok_dev, model_width)
    back_middle = upstream + norm_back(back_mlp_in * (1.0 + scale_mlp), normed_mlp, spread_mlp)
    back_att = back_middle * gate_att
    back_att_b = back_att.astype(jnp.bfloat16).reshape(row_count, model_width)
    mat_out = collect_again(out_weight)
    grad_outw = spread_grad(attended_b, back_att_b)
    sum_outb = jnp.sum(back_att, axis=(0, 1))
    back_attended = jnp.einsum(
        "rd,cd->rc", back_att_b, mat_out, preferred_element_type=jnp.float32
    ).astype(jnp.bfloat16)
    back_attended = back_attended.reshape(slot_total, tok_dev, H, HD)
    back_probs = jnp.einsum(
        "sqhd,skhd->shqk", back_attended, values_heads, preferred_element_type=jnp.float32
    )
    row_delta = jnp.einsum("sqhd,sqhd->shq", back_attended.astype(jnp.float32), attended)[..., None]
    back_scores = (attn_probs * (back_probs - row_delta) * scale).astype(jnp.bfloat16)
    back_queries = jnp.einsum(
        "shqk,skhd->sqhd", back_scores, keys_heads, preferred_element_type=jnp.float32
    )
    key_terms = jnp.einsum(
        "shqk,sqhd->skhd", back_scores, queries, preferred_element_type=jnp.float32
    ).reshape(slot_total, -1, model_width)
    value_terms = jnp.einsum(
        "shqk,sqhd->skhd", probs_b, back_attended, preferred_element_type=jnp.float32
    ).reshape(slot_total, -1, model_width)
    back_keys, back_values = (
        lax.psum_scatter(key_terms, "seq", scatter_dimension=1, tiled=True),
        lax.psum_scatter(value_terms, "seq", scatter_dimension=1, tiled=True),
    )
    back_qkv = jnp.concatenate(
        [
            back_queries.reshape(row_count, model_width),
            back_keys.reshape(row_count, model_width),
            back_values.reshape(row_count, model_width),
        ],
        axis=1,
    )
    back_qkv_b = back_qkv.astype(jnp.bfloat16)
    mat_qkv = collect_again(qkv_weight)
    grad_qkvw = spread_grad(attn_in, back_qkv_b)
    sum_qkvb = jnp.sum(back_qkv, axis=0)
    back_attn_in = jnp.einsum(
        "rd,cd->rc", back_qkv_b, mat_qkv, preferred_element_type=jnp.float32
    ).reshape(slot_total, tok_dev, model_width)
    latent_gradient = jnp.where(
        live_mask,
        back_middle + norm_back(back_attn_in * (1.0 + scale_att), normed_att, spread_att),
        0.0,
    )
    slot_modgrad = jnp.concatenate(
        [
            jnp.sum(back_attn_in, axis=1),
            jnp.sum(back_attn_in * normed_att, axis=1),
            jnp.sum(back_middle * branch_att, axis=1),
            jnp.sum(back_mlp_in, axis=1),
            jnp.sum(back_mlp_in * normed_mlp, axis=1),
            jnp.sum(upstream * branch_mlp, axis=1),
        ],
        axis=1,
    )
    modgrad_table = jnp.dot(slot_matches.T, slot_modgrad, precision=lax.Precision.HIGHEST)
    modgrad_cols = lax.psum_scatter(modgrad_table, ("dp", "seq"), scatter_dimension=1, tiled=True)
    grad_adaw = jnp.dot(
        rounded(jax.nn.silu(condition)).T, modgrad_cols, precision=lax.Precision.HIGHEST
    )
    grad_adab = jnp.sum(modgrad_cols, axis=0)
    cond_term = jnp.dot(modgrad_cols, rounded(ada_weight).T, precision=lax.Precision.HIGHEST)
    cond_sum, total_qkvb, total_outb, total_upb, total_downb = lax.psum(
        (cond_term, sum_qkvb, sum_outb, sum_upb, sum_downb), ("dp", "seq")
    )
    condition_grad = cond_sum * silu_slope(condition)
    seq_index = lax.axis_index("seq")

    def own_part(full_sum, local_bias):
        length = local_bias.shape[0]
        return lax.dynamic_slice_in_dim(full_sum, seq_index * length, length)

    grad_qkvb = own_part(total_qkvb, qkv_bias)
    grad_outb = own_part(total_outb, out_bias)
    grad_upb = own_part(total_upb, up_bias)
    grad_downb = own_part(total_downb, down_bias)
    grads_all = (
        grad_adaw,
        grad_adab,
        grad_qkvw,
        grad_qkvb,
        grad_outw,
        grad_outb,
        grad_upw,
        grad_upb,
        grad_downw,
        grad_downb,
    )
    params_all = (
        ada_weight,
        ada_bias,
        qkv_weight,
        qkv_bias,
        out_weight,
        out_bias,
        up_weight,
        up_bias,
        down_weight,
        down_bias,
    )
    means_all = (
        mean_adaw,
        mean_adab,
        mean_qkvw,
        mean_qkvb,
        mean_outw,
        mean_outb,
        mean_upw,
        mean_upb,
        mean_downw,
        mean_downb,
    )
    squares_all = (
        sqmean_adaw,
        sqmean_adab,
        sqmean_qkvw,
        sqmean_qkvb,
        sqmean_outw,
        sqmean_outb,
        sqmean_upw,
        sqmean_upb,
        sqmean_downw,
        sqmean_downb,
    )
    updates = [
        adamw_step(p_item, g_item, m_item, v_item)
        for p_item, g_item, m_item, v_item in zip(params_all, grads_all, means_all, squares_all)
    ]
    newvals = tuple((entry[0] for entry in updates))
    newmeans = tuple((entry[1] for entry in updates))
    newsqrs = tuple((entry[2] for entry in updates))
    return (
        (block_output, latent_gradient, condition_grad) + grads_all + newvals + newmeans + newsqrs
    )


def solution(mesh):
    return jax.shard_map(
        on_device,
        mesh=mesh,
        in_specs=(
            P("dp", "seq", None),
            P(),
            P("dp", None),
            P("dp"),
            P("dp", "seq", None),
            P(None, ("dp", "seq")),
            P(("dp", "seq")),
            P("dp", "seq"),
            P("seq"),
            P("dp", "seq"),
            P("seq"),
            P("dp", "seq"),
            P("seq"),
            P("dp", "seq"),
            P("seq"),
            P(None, ("dp", "seq")),
            P(("dp", "seq")),
            P("dp", "seq"),
            P("seq"),
            P("dp", "seq"),
            P("seq"),
            P("dp", "seq"),
            P("seq"),
            P("dp", "seq"),
            P("seq"),
            P(None, ("dp", "seq")),
            P(("dp", "seq")),
            P("dp", "seq"),
            P("seq"),
            P("dp", "seq"),
            P("seq"),
            P("dp", "seq"),
            P("seq"),
            P("dp", "seq"),
            P("seq"),
        ),
        out_specs=(
            P("dp", "seq", None),
            P("dp", "seq", None),
            P(),
            P(None, ("dp", "seq")),
            P(("dp", "seq")),
            P("dp", "seq"),
            P("seq"),
            P("dp", "seq"),
            P("seq"),
            P("dp", "seq"),
            P("seq"),
            P("dp", "seq"),
            P("seq"),
            P(None, ("dp", "seq")),
            P(("dp", "seq")),
            P("dp", "seq"),
            P("seq"),
            P("dp", "seq"),
            P("seq"),
            P("dp", "seq"),
            P("seq"),
            P("dp", "seq"),
            P("seq"),
            P(None, ("dp", "seq")),
            P(("dp", "seq")),
            P("dp", "seq"),
            P("seq"),
            P("dp", "seq"),
            P("seq"),
            P("dp", "seq"),
            P("seq"),
            P("dp", "seq"),
            P("seq"),
            P(None, ("dp", "seq")),
            P(("dp", "seq")),
            P("dp", "seq"),
            P("seq"),
            P("dp", "seq"),
            P("seq"),
            P("dp", "seq"),
            P("seq"),
            P("dp", "seq"),
            P("seq"),
        ),
        check_vma=False,
    )
```

profile of v0, /device:TPU:0, one launch (start us, length us, event | category | flops | bytes accessed | tf_op | source)
XLA Modules:
  0.0 1488.3 jit_solution(5045543389649155626)
XLA Ops:
  8.4 10.0 all-gather.3
  20.1 5.4 all-gather.4
  26.6 8.7 all_gather.62
  37.1 70.0 %all-gather.2 = f32[32,216,8]{1,2,0:T(8,128)S(1)} all-gather(f32[1,216,8]{1,2,0:T(8,128)S(1)} %fusion.10), channel_id=1, replica_groups=mesh['dp'=16,'seq'=2] {'dp','seq'}, dimensions={0}, use_global_device_ids=true | all-gather | bytes 228096 | tf_op jit(solution)/shard_map/all_gather | solution.py:136
  111.4 7.3 all-reduce.7
  118.7 4.4 all-gather.5
  125.1 4.8 fusion.1
  129.9 8.0 all-gather
  139.9 7.7 all-gather.1
  147.8 2.2 fusion.94
  152.9 3.3 fusion.92
  157.0 71.1 %all-gather.16.cloned.1.call-done = bf16[1152,4608]{1,0:T(8,128)(2,1)} async-done(((bf16[72,4608]{1,0:T(8,128)(2,1)}), bf16[1152,4608]{1,0:T(8,128)(2,1)}) %all-gather.16.cloned.1.call-update) | async-done | bytes 10616848 | tf_op jit(solution)/shard_map/all_gather | solution.py:72
  228.0 5.9 convolution_add_fusion
  233.9 8.7 fusion.45
  242.7 211.9 %reduce-scatter.30.cloned.1.call-done = f32[288,1152]{1,0:T(8,128)} async-done(((f32[4608,1152]{1,0:T(8,128)}), f32[288,1152]{1,0:T(8,128)}) %reduce-scatter.30.cloned.1.call-update) | async-done | bytes 1327120 | tf_op jit(solution)/shard_map/reduce_scatter | solution.py:82
  454.6 3.1 copy.116
  457.8 27.5 %reduce-scatter.36.cloned.1.call-done = f32[576,288]{1,0:T(8,128)} async-done(((f32[1152,288]{1,0:T(8,128)}), f32[576,288]{1,0:T(8,128)}) %reduce-scatter.36.cloned.1.call-update) | async-done | bytes 663568
  485.3 2.3 copy.117
  487.7 3.6 divide_subtract_fusion.1
  491.3 10.8 all-gather.6
  502.1 1.4 copy.100
  503.5 2.8 reshape.400
  507.9 87.0 %all-gather.18.cloned.1.call-done = bf16[4608,1152]{1,0:T(8,128)(2,1)} async-done(((bf16[288,1152]{1,0:T(8,128)(2,1)}), bf16[4608,1152]{1,0:T(8,128)(2,1)}) %all-gather.18.cloned.1.call-update) | async-done | bytes 10616848 | tf_op jit(solution)/shard_map/all_gather | solution.py:72
  594.9 8.7 fusion.95
  603.7 8.6 fusion.17
  613.0 3.8 multiply_reduce_fusion.4
  620.3 2.7 multiply_convert_fusion.1
  625.1 15.3 %reduce-scatter.24.cloned.1.call-done = f32[1,128,1152]{1,2,0:T(8,128)} async-done(((f32[1,256,1152]{1,2,0:T(8,128)}), f32[1,128,1152]{1,2,0:T(8,128)}) %reduce-scatter.24.cloned.1.call-update) | async-done | bytes 589840 | tf_op jit(solution)/shard_map/reduce_scatter | solution.py:231
  640.4 24.1 %reduce-scatter.22.cloned.1.call-done = f32[1,128,1152]{1,2,0:T(8,128)} async-done(((f32[1,256,1152]{1,2,0:T(8,128)}), f32[1,128,1152]{1,2,0:T(8,128)}) %reduce-scatter.22.cloned.1.call-update) | async-done | bytes 589840 | tf_op jit(solution)/shard_map/reduce_scatter | solution.py:230
  664.5 6.8 fusion.19
  673.3 3.2 fusion.42
  677.6 9.1 fusion.71
  686.7 11.5 fusion.29
  700.4 97.5 %all-reduce.11.cloned.1.call-done = f32[8,6912]{1,0:T(8,128)} async-done(((f32[8,6912]{1,0:T(8,128)}), f32[8,6912]{1,0:T(8,128)}) %all-reduce.11.cloned.1.call-update) | async-done | bytes 221200
  797.9 2.1 fusion.52
  800.0 80.8 %reduce-scatter.40.cloned.1.call-done = f32[72,1152]{1,0:T(8,128)} async-done(((f32[1152,1152]{1,0:T(8,128)}), f32[72,1152]{1,0:T(8,128)}) %reduce-scatter.40.cloned.1.call-update) | async-done | bytes 331792
  880.8 2.0 copy.114
  883.0 171.3 %reduce-scatter.38.cloned.1.call-done = f32[72,3456]{1,0:T(8,128)} async-done(((f32[1152,3456]{1,0:T(8,128)}), f32[72,3456]{1,0:T(8,128)}) %reduce-scatter.38.cloned.1.call-update) | async-done | bytes 995344
  1054.3 3.0 copy.112
  1059.4 211.5 %reduce-scatter.26.cloned.1.call-done = f32[72,4608]{1,0:T(8,128)} async-done(((f32[1152,4608]{1,0:T(8,128)}), f32[72,4608]{1,0:T(8,128)}) %reduce-scatter.26.cloned.1.call-update) | async-done | bytes 1327120 | tf_op jit(solution)/shard_map/reduce_scatter | solution.py:82
  1271.7 4.9 divide_subtract_fusion
  1276.6 125.8 %all-reduce.13.cloned.1.call-done = (f32[8,1152]{1,0:T(8,128)}, f32[3456]{0:T(1024)}, f32[1152]{0:T(1024)}, f32[4608]{0:T(1024)}, f32[1152]{0:T(1024)}) async-done(((f32[8,1152]{1,0:T(8,128)}, f32[3456]{0:T(1024)}, f32[1152]{0:T(1024)}, f32[4608]{0:T(1024)}, f32[1152]{0:T(1024)}), (f32[8,1152]{1,0:T(8,128)}, f32[3456]{0:T(1024)}, f32[1152]{0:T(1024)}, f32[4608]{0:T(1024)}, ...) | async-done | bytes 78352 | tf_op jit(solution)/shard_map/psum | solution.py:271
  1409.5 12.6 reduce-scatter.34.cloned.1.call-done
  1424.1 28.4 %reduce-scatter.32.cloned.1.call-done = f32[1728,72]{1,0:T(8,128)} async-done(((f32[3456,72]{1,0:T(8,128)}), f32[1728,72]{1,0:T(8,128)}) %reduce-scatter.32.cloned.1.call-update) | async-done | bytes 497680
  1452.5 1.6 copy.113
  1454.2 2.7 divide_subtract_fusion.3
  1456.9 21.8 %reduce-scatter.28.cloned.1.call-done = f32[72,2304]{1,0:T(8,128)} async-done(((f32[72,4608]{1,0:T(8,128)}), f32[72,2304]{1,0:T(8,128)}) %reduce-scatter.28.cloned.1.call-update) | async-done | bytes 663568 | tf_op jit(solution)/shard_map/reduce_scatter | solution.py:83
  1478.7 2.6 divide_subtract_fusion.2
  (288 shorter events, 39.8 us)
Async XLA Ops:
  7.2 117.8 %all-gather.12.cloned.1.call-start = ((), (), s32[]{:S(2)}) async-start(), calls=%async_computation.10 | async-start | bytes 8460288 | tf_op jit(solution)/shard_map/all_gather | solution.py:72
  20.0 132.9 %all-gather.14.cloned.1.call-start = ((), (), s32[]{:S(2)}) async-start(), calls=%async_computation.11 | async-start | bytes 2820096 | tf_op jit(solution)/shard_map/all_gather | solution.py:72
  26.4 201.6 %all-gather.16.cloned.1.call-start = ((), (), s32[]{:S(2)}) async-start(), calls=%async_computation.12 | async-start | bytes 11280384 | tf_op jit(solution)/shard_map/all_gather | solution.py:72
  26.5 82.2 %copy-start.62 = (f32[576]{0:T(1024)S(1)}, f32[576]{0:T(1024)}, u32[]{:S(2)}) copy-start(f32[576]{0:T(1024)} %param.45) | copy-start | bytes 6916
  26.6 82.2 %copy-start.84 = (u32[32]{0:T(128)S(1)}, u32[32]{0:T(128)}, u32[]{:S(2)}) copy-start(u32[32]{0:T(128)} %constant.88) | copy-start | bytes 388
  26.6 84.1 %copy-start.64 = (f32[576]{0:T(1024)S(1)}, f32[576]{0:T(1024)}, u32[]{:S(2)}) copy-start(f32[576]{0:T(1024)} %param.49) | copy-start | bytes 6916
  26.6 92.1 %copy-start.43 = (f32[2304]{0:T(1024)S(1)}, f32[2304]{0:T(1024)}, u32[]{:S(2)}) copy-start(f32[2304]{0:T(1024)} %param.47) | copy-start | bytes 27652
  35.3 88.5 %copy-start = (f32[1,128,1152]{2,1,0:T(8,128)S(1)}, f32[1,128,1152]{2,1,0:T(8,128)}, u32[]{:S(2)}) copy-start(f32[1,128,1152]{2,1,0:T(8,128)} %param.35) | copy-start | bytes 1769476
  35.3 419.3 %reduce-scatter.30.cloned.1.call-start = ((), (), s32[]{:S(2)}) async-start(), calls=%async_computation.18 | async-start | bytes 22560768 | tf_op jit(solution)/shard_map/reduce_scatter | solution.py:82
  242.7 242.6 %reduce-scatter.36.cloned.1.call-start = ((), (), s32[]{:S(2)}) async-start(), calls=%async_computation.21 | async-start | bytes 2654208
  457.8 137.1 %all-gather.18.cloned.1.call-start = ((), (), s32[]{:S(2)}) async-start(), calls=%async_computation.13 | async-start | bytes 11280384 | tf_op jit(solution)/shard_map/all_gather | solution.py:72
  506.3 134.0 %reduce-scatter.24.cloned.1.call-start = ((), (), s32[]{:S(2)}) async-start(), calls=%async_computation.15 | async-start | bytes 1769472 | tf_op jit(solution)/shard_map/reduce_scatter | solution.py:231
  620.1 44.3 %reduce-scatter.22.cloned.1.call-start = ((), (), s32[]{:S(2)}) async-start(), calls=%async_computation.14 | async-start | bytes 1769472 | tf_op jit(solution)/shard_map/reduce_scatter | solution.py:230
  624.5 173.4 %all-reduce.11.cloned.1.call-start = ((), (), s32[]{:S(2)}) async-start(), calls=%async_computation.22 | async-start | bytes 442368
  673.0 207.8 %reduce-scatter.40.cloned.1.call-start = ((), (), s32[]{:S(2)}) async-start(), calls=%async_computation.24 | async-start | bytes 5640192
  676.5 377.8 %reduce-scatter.38.cloned.1.call-start = ((), (), s32[]{:S(2)}) async-start(), calls=%async_computation.23 | async-start | bytes 16920576
  686.7 584.2 %reduce-scatter.26.cloned.1.call-start = ((), (), s32[]{:S(2)}) async-start(), calls=%async_computation.16 | async-start | bytes 22560768 | tf_op jit(solution)/shard_map/reduce_scatter | solution.py:82
  698.2 704.2 %all-reduce.13.cloned.1.call-start = ((), (), s32[]{:S(2)}) async-start(), calls=%async_computation.25 | async-start | bytes 180224 | tf_op jit(solution)/shard_map/psum | solution.py:271
  800.0 622.1 %reduce-scatter.34.cloned.1.call-start = ((), (), s32[]{:S(2)}) async-start(), calls=%async_computation.20 | async-start | bytes 884736
  882.9 174.6 %copy-start.82 = (f32[128]{0:T(128)S(1)}, f32[128]{0:T(128)}, u32[]{:S(2)}) copy-start(f32[128]{0:T(128)} %get-tuple-element.46) | copy-start | bytes 1540
  882.9 174.6 %copy-start.83 = (f32[128]{0:T(128)S(1)}, f32[128]{0:T(128)}, u32[]{:S(2)}) copy-start(f32[128]{0:T(128)} %get-tuple-element.54) | copy-start | bytes 1540
  882.9 174.6 %copy-start.57 = (f32[128]{0:T(128)S(1)}, f32[128]{0:T(128)}, u32[]{:S(2)}) copy-start(f32[128]{0:T(128)} %copy-done.55) | copy-start | bytes 1540
  882.9 174.6 %copy-start.61 = (f32[128]{0:T(128)S(1)}, f32[128]{0:T(128)}, u32[]{:S(2)}) copy-start(f32[128]{0:T(128)} %copy-done.59) | copy-start | bytes 1540
  882.9 569.6 %reduce-scatter.32.cloned.1.call-start = ((), (), s32[]{:S(2)}) async-start(), calls=%async_computation.19 | async-start | bytes 2654208
  1057.3 213.6 %copy-start.79 = (f32[216]{0:T(256)S(1)}, f32[216]{0:T(256)}, u32[]{:S(2)}) copy-start(f32[216]{0:T(256)} %param.41) | copy-start | bytes 2596
  1057.3 213.6 %copy-start.80 = (f32[216]{0:T(256)S(1)}, f32[216]{0:T(256)}, u32[]{:S(2)}) copy-start(f32[216]{0:T(256)} %param.51) | copy-start | bytes 2596
  1057.3 213.6 %copy-start.81 = (f32[216]{0:T(256)S(1)}, f32[216]{0:T(256)}, u32[]{:S(2)}) copy-start(f32[216]{0:T(256)} %param.61) | copy-start | bytes 2596
  1057.3 214.2 %copy-start.14 = (f32[1152,216]{0,1:T(8,128)S(1)}, f32[1152,216]{0,1:T(8,128)}, u32[]{:S(2)}) copy-start(f32[1152,216]{0,1:T(8,128)} %param.40) | copy-start | bytes 2985988
  1057.3 214.2 %copy-start.36 = (bf16[8,1152]{1,0:T(8,128)(2,1)S(1)}, bf16[8,1152]{1,0:T(8,128)(2,1)}, u32[]{:S(2)}) copy-start(bf16[8,1152]{1,0:T(8,128)(2,1)} %copy-done.35) | copy-start | bytes 55300
  1057.4 421.3 %reduce-scatter.28.cloned.1.call-start = ((), (), s32[]{:S(2)}) async-start(), calls=%async_computation.17 | async-start | bytes 1990656 | tf_op jit(solution)/shard_map/reduce_scatter | solution.py:83
  1059.4 217.2 %copy-start.73 = (f32[216]{0:T(256)}, f32[216]{0:T(256)S(1)}, u32[]{:S(2)}) copy-start(f32[216]{0:T(256)S(1)} %dynamic-slice_reduce_fusion) | copy-start | bytes 2596
  1271.5 130.9 %copy-start.63 = (f32[576]{0:T(1024)S(1)}, f32[576]{0:T(1024)}, u32[]{:S(2)}) copy-start(f32[576]{0:T(1024)} %param.45) | copy-start | bytes 6916
  1271.5 130.9 %copy-start.74 = (f32[576]{0:T(1024)S(1)}, f32[576]{0:T(1024)}, u32[]{:S(2)}) copy-start(f32[576]{0:T(1024)} %param.55) | copy-start | bytes 6916
  1271.6 130.9 %copy-start.75 = (f32[576]{0:T(1024)S(1)}, f32[576]{0:T(1024)}, u32[]{:S(2)}) copy-start(f32[576]{0:T(1024)} %param.65) | copy-start | bytes 6916
  1271.6 132.3 %copy-start.65 = (f32[576]{0:T(1024)S(1)}, f32[576]{0:T(1024)}, u32[]{:S(2)}) copy-start(f32[576]{0:T(1024)} %param.49) | copy-start | bytes 6916
  1271.6 132.3 %copy-start.76 = (f32[576]{0:T(1024)S(1)}, f32[576]{0:T(1024)}, u32[]{:S(2)}) copy-start(f32[576]{0:T(1024)} %param.59) | copy-start | bytes 6916
  1271.6 132.2 %copy-start.77 = (f32[576]{0:T(1024)S(1)}, f32[576]{0:T(1024)}, u32[]{:S(2)}) copy-start(f32[576]{0:T(1024)} %param.69) | copy-start | bytes 6916
  1271.6 133.6 %copy-start.51 = (f32[1728]{0:T(1024)S(1)}, f32[1728]{0:T(1024)}, u32[]{:S(2)}) copy-start(f32[1728]{0:T(1024)} %param.43) | copy-start | bytes 20740
  1271.6 133.6 %copy-start.71 = (f32[1728]{0:T(1024)S(1)}, f32[1728]{0:T(1024)}, u32[]{:S(2)}) copy-start(f32[1728]{0:T(1024)} %param.53) | copy-start | bytes 20740
  1271.6 133.6 %copy-start.72 = (f32[1728]{0:T(1024)S(1)}, f32[1728]{0:T(1024)}, u32[]{:S(2)}) copy-start(f32[1728]{0:T(1024)} %param.63) | copy-start | bytes 20740
  1271.6 135.0 %copy-start.44 = (f32[2304]{0:T(1024)S(1)}, f32[2304]{0:T(1024)}, u32[]{:S(2)}) copy-start(f32[2304]{0:T(1024)} %param.47) | copy-start | bytes 27652
  1271.6 135.0 %copy-start.66 = (f32[2304]{0:T(1024)S(1)}, f32[2304]{0:T(1024)}, u32[]{:S(2)}) copy-start(f32[2304]{0:T(1024)} %param.57) | copy-start | bytes 27652
  1271.7 135.0 %copy-start.67 = (f32[2304]{0:T(1024)S(1)}, f32[2304]{0:T(1024)}, u32[]{:S(2)}) copy-start(f32[2304]{0:T(1024)} %param.67) | copy-start | bytes 27652
  1271.7 136.4 %copy-start.38 = (f32[8,1152]{1,0:T(8,128)S(1)}, f32[8,1152]{1,0:T(8,128)}, u32[]{:S(2)}) copy-start(f32[8,1152]{1,0:T(8,128)} %param.36) | copy-start | bytes 110596
  1271.7 151.5 %copy-start.26 = (f32[72,576]{1,0:T(8,128)S(1)}, f32[72,576]{1,0:T(8,128)}, u32[]{:S(2)}) copy-start(f32[72,576]{1,0:T(8,128)} %param.44) | copy-start | bytes 497668
  1271.7 151.5 %copy-start.33 = (f32[72,576]{1,0:T(8,128)S(1)}, f32[72,576]{1,0:T(8,128)}, u32[]{:S(2)}) copy-start(f32[72,576]{1,0:T(8,128)} %param.54) | copy-start | bytes 497668
  1271.7 151.5 %copy-start.34 = (f32[72,576]{1,0:T(8,128)S(1)}, f32[72,576]{1,0:T(8,128)}, u32[]{:S(2)}) copy-start(f32[72,576]{1,0:T(8,128)} %param.64) | copy-start | bytes 497668
  1276.6 177.6 %copy-start.23 = (f32[72,1728]{1,0:T(8,128)S(1)}, f32[72,1728]{1,0:T(8,128)}, u32[]{:S(2)}) copy-start(f32[72,1728]{1,0:T(8,128)} %param.42) | copy-start | bytes 1492996
  (56 other events, 706.1 us)
Sparse Core Ops, SparseCore 0:
  20.1 73.9 all-gather.11
  96.8 41.6 all-gather.13
  140.8 87.1 all-gather.15
  242.8 211.7 reduce-scatter.29
  457.9 27.4 reduce-scatter.35
  506.5 88.3 all-gather.17
  620.3 20.0 reduce-scatter.23
  642.6 21.8 reduce-scatter.21
  673.1 124.7 all-reduce.10
  801.8 79.0 reduce-scatter.39
  885.0 169.3 reduce-scatter.37
  1058.3 212.5 reduce-scatter.25
  1279.0 123.3 all-reduce.12
  1405.1 16.9 reduce-scatter.33
  1424.2 28.3 reduce-scatter.31
  1455.2 23.4 reduce-scatter.27
where the time goes:
time: 1490 us
  waiting for transfers between devices  1190 us (80%)
  blocking collectives  132 us (9%)
  matrix products  92 us (6%)
  local copies, waits for them, and re-layouts  30.4 us (2%)
  other arithmetic  27.4 us (2%)
  between operations  18.2 us (1%)
    reduce_scatter x2, waiting for transfers between devices, spread_grad(): lax.psum_scatter(term, 'dp', scatter_dimension=0, tiled=True)  423 us
    unnamed x22, waiting for transfers between devices  418 us
    all_gather x4, waiting for transfers between devices, collect(): lax.all_gather(pieces, 'dp', axis=0, tiled=True)  158 us
    psum x1, waiting for transfers between devices, on_device(): lax.psum((cond_term, sum_qkvb, sum_outb, sum_upb, sum_downb), ('dp', 'seq'))  126 us
    all_gather x1, blocking collectives, on_device(): modulation = lax.all_gather(mod_cols, ('dp', 'seq'), axis=1, tiled=True)  70 us
    all_gather x4, blocking collectives, collect(): lax.all_gather(weight.astype(jnp.bfloat16), 'seq', axis=1, tiled=True)  34.8 us
    dot_general x4, matrix products, spread_grad(): jnp.einsum('rc,rd->cd', left, right, preferred_element_type=jnp.float32)  32.5 us
  transfers between devices with their start and end apart: 16, of which 14 were waited for; matrix products, arithmetic and copies ran while one was open for 5% of the time, Pallas kernels for 0%

commit v1 on v0

--- a/solution.py
+++ b/solution.py
@@ -64,23 +64,98 @@
     )
 
 
-def collect(weight, bias):
-    pieces, bias_full = (
-        lax.all_gather(weight.astype(jnp.bfloat16), "seq", axis=1, tiled=True),
-        lax.all_gather(bias.astype(jnp.bfloat16), "seq", axis=0, tiled=True),
-    )
-    return (lax.all_gather(pieces, "dp", axis=0, tiled=True), bias_full.astype(jnp.float32))
-
-
-def collect_again(weight):
-    pieces = lax.all_gather(weight.astype(jnp.bfloat16), "seq", axis=1, tiled=True)
-    return lax.all_gather(pieces, "dp", axis=0, tiled=True)
-
-
-def spread_grad(left, right):
-    term = jnp.einsum("rc,rd->cd", left, right, preferred_element_type=jnp.float32)
-    partial_value = lax.psum_scatter(term, "dp", scatter_dimension=0, tiled=True)
-    return lax.psum_scatter(partial_value, "seq", scatter_dimension=1, tiled=True)
+def flat_index(axes):
+    index = lax.axis_index(axes[0])
+    for axis in axes[1:]:
+        index = index * lax.axis_size(axis) + lax.axis_index(axis)
+    return index
+
+
+def swap_bit(values, axes, step):
+    total = 1
+    for axis in axes:
+        total *= lax.axis_size(axis)
+    return lax.ppermute(values, axes, [(i, i ^ step) for i in range(total)])
+
+
+def axes_size(axes):
+    total = 1
+    for axis in axes:
+        total *= lax.axis_size(axis)
+    return total
+
+
+def gather_tree(values, axes):
+    index, blocks, step = flat_index(axes), values[None], 1
+    while step < axes_size(axes):
+        other = swap_bit(blocks, axes, step)
+        upper = (index // step) % 2 == 1
+        blocks = jnp.concatenate(
+            [jnp.where(upper, other, blocks), jnp.where(upper, blocks, other)], axis=0
+        )
+        step *= 2
+    return blocks
+
+
+def scatter_tree(blocks, axes, sent=None):
+    index, step = flat_index(axes), axes_size(axes) // 2
+    while step >= 1:
+        low, high = blocks[:step], blocks[step:]
+        upper = (index // step) % 2 == 1
+        away = jnp.where(upper, low, high)
+        if sent is not None:
+            away = away.astype(sent)
+        kept = jnp.where(upper, high, low)
+        blocks = kept + swap_bit(away, axes, step).astype(kept.dtype)
+        step //= 2
+    return blocks[0]
+
+
+def sum_tree(values, axes):
+    step = 1
+    while step < axes_size(axes):
+        values = values + swap_bit(values, axes, step)
+        step *= 2
+    return values
+
+
+def join_columns(halves, widths):
+    parts, start = [], 0
+    for width in widths:
+        part = halves[:, :, start : start + width]
+        parts.append(jnp.moveaxis(part, 0, 1).reshape(part.shape[1], -1))
+        start += width
+    return parts
+
+
+def split_columns(parts):
+    ways = lax.axis_size("seq")
+    blocks = [
+        jnp.moveaxis(part.reshape(part.shape[0], ways, -1), 1, 0) for part in parts
+    ]
+    return jnp.concatenate(blocks, axis=2)
+
+
+def weight_term(left, right):
+    return jnp.einsum("rc,rd->cd", left, right, preferred_element_type=jnp.float32).astype(
+        jnp.bfloat16
+    )
+
+
+def spread_terms(terms):
+    widths = [term.shape[1] // lax.axis_size("seq") for term in terms]
+    joined = jnp.concatenate(terms, axis=1) if len(terms) > 1 else terms[0]
+    rows = lax.psum_scatter(joined, "dp", scatter_dimension=0, tiled=True)
+    pieces, start = [], 0
+    for term in terms:
+        pieces.append(rows[:, start : start + term.shape[1]])
+        start += term.shape[1]
+    own = scatter_tree(split_columns(pieces).astype(jnp.float32), ("seq",), jnp.bfloat16)
+    blocks, start = [], 0
+    for width in widths:
+        blocks.append(own[:, start : start + width])
+        start += width
+    return blocks
 
 
 def on_device(
@@ -133,11 +208,33 @@
     mod_cols = jnp.dot(
         silu_cond, ada_weight.astype(jnp.bfloat16), preferred_element_type=jnp.float32
     ) + rounded(ada_bias)
-    modulation = lax.all_gather(mod_cols, ("dp", "seq"), axis=1, tiled=True)
+    modulation = jnp.moveaxis(gather_tree(mod_cols, ("dp", "seq")), 0, 1).reshape(
+        latent_count, -1
+    )
     slot_mod = jnp.dot(slot_matches, modulation, precision=lax.Precision.HIGHEST)[:, None, :]
     shift_att, scale_att, gate_att, shift_mlp, scale_mlp, gate_mlp = jnp.split(slot_mod, 6, axis=2)
     upstream = jnp.where(live_mask, output_gradient, 0.0)
-    mat_qkv, vec_qkv = collect(qkv_weight, qkv_bias)
+    biases = (qkv_bias, out_bias, up_bias, down_bias)
+    bias_rows = gather_tree(
+        jnp.concatenate(biases).astype(jnp.bfloat16)[None], ("seq",)
+    )
+    vec_qkv, vec_out, vec_up, vec_down = (
+        part[0].astype(jnp.float32)
+        for part in join_columns(bias_rows, [item.shape[0] for item in biases])
+    )
+    wide = (qkv_weight, out_weight, up_weight)
+    wide_halves = gather_tree(jnp.concatenate(wide, axis=1).astype(jnp.bfloat16), ("seq",))
+    wide_rows = jnp.concatenate(
+        join_columns(wide_halves, [item.shape[1] for item in wide]), axis=1
+    )
+    wide_full = lax.all_gather(wide_rows, "dp", axis=0, tiled=True)
+    qkv_end = 3 * model_width
+    mat_qkv = wide_full[:, :qkv_end]
+    mat_out = wide_full[:, qkv_end : qkv_end + model_width]
+    mat_up = wide_full[:, qkv_end + model_width :]
+    down_halves = gather_tree(down_weight.astype(jnp.bfloat16), ("seq",))
+    down_rows = join_columns(down_halves, [down_weight.shape[1]])[0]
+    mat_down = lax.all_gather(down_rows, "dp", axis=0, tiled=True)
     normed_att, spread_att = normalize(latents)
     attn_in = (
         (normed_att * (1.0 + scale_att) + shift_att)
@@ -150,10 +247,10 @@
     queries = qkv_all[:, :model_width].reshape(slot_total, tok_dev, H, HD)
     keys_own = qkv_all[:, model_width : 2 * model_width].reshape(slot_total, tok_dev, model_width)
     values_own = qkv_all[:, 2 * model_width :].reshape(slot_total, tok_dev, model_width)
-    keys_all, values_all = (
-        lax.all_gather(keys_own, "seq", axis=1, tiled=True),
-        lax.all_gather(values_own, "seq", axis=1, tiled=True),
-    )
+    pairs_own = jnp.concatenate([keys_own, values_own], axis=2)
+    pairs_all = jnp.moveaxis(gather_tree(pairs_own, ("seq",)), 0, 1)
+    pairs_all = pairs_all.reshape(slot_total, -1, 2 * model_width)
+    keys_all, values_all = pairs_all[:, :, :model_width], pairs_all[:, :, model_width:]
     keys_heads = keys_all.reshape(slot_total, -1, H, HD)
     values_heads = values_all.reshape(slot_total, -1, H, HD)
     scores = (
@@ -168,7 +265,6 @@
         "shqk,skhd->sqhd", probs_b, values_heads, preferred_element_type=jnp.float32
     )
     attended_b = attended.reshape(row_count, model_width).astype(jnp.bfloat16)
-    mat_out, vec_out = collect(out_weight, out_bias)
     branch_att = (
         jnp.dot(attended_b, mat_out, preferred_element_type=jnp.float32) + vec_out
     ).reshape(slot_total, tok_dev, model_width)
@@ -179,25 +275,22 @@
         .astype(jnp.bfloat16)
         .reshape(row_count, model_width)
     )
-    mat_up, vec_up = collect(up_weight, up_bias)
     hidden = jnp.dot(mlp_in, mat_up, preferred_element_type=jnp.float32) + vec_up
     activated = gelu_tanh(hidden).astype(jnp.bfloat16)
-    mat_down, vec_down = collect(down_weight, down_bias)
+    activated, mat_down = lax.optimization_barrier((activated, mat_down))
     branch_mlp = (
         jnp.dot(activated, mat_down, preferred_element_type=jnp.float32) + vec_down
     ).reshape(slot_total, tok_dev, model_width)
     block_output = jnp.where(live_mask, middle + gate_mlp * branch_mlp, 0.0)
-    mat_down = collect_again(down_weight)
     back_down = upstream * gate_mlp
     back_down_b = back_down.astype(jnp.bfloat16).reshape(row_count, model_width)
-    grad_downw = spread_grad(activated, back_down_b)
+    (grad_downw,) = spread_terms([weight_term(activated, back_down_b)])
     sum_downb = jnp.sum(back_down, axis=(0, 1))
     back_hidden = jnp.einsum(
         "rd,fd->rf", back_down_b, mat_down, preferred_element_type=jnp.float32
     ) * gelu_slope(hidden)
     back_hidden_b = back_hidden.astype(jnp.bfloat16)
-    mat_up = collect_again(up_weight)
-    grad_upw = spread_grad(mlp_in, back_hidden_b)
+    term_up = weight_term(mlp_in, back_hidden_b)
     sum_upb = jnp.sum(back_hidden, axis=0)
     back_mlp_in = jnp.einsum(
         "rf,cf->rc", back_hidden_b, mat_up, preferred_element_type=jnp.float32
@@ -205,8 +298,7 @@
     back_middle = upstream + norm_back(back_mlp_in * (1.0 + scale_mlp), normed_mlp, spread_mlp)
     back_att = back_middle * gate_att
     back_att_b = back_att.astype(jnp.bfloat16).reshape(row_count, model_width)
-    mat_out = collect_again(out_weight)
-    grad_outw = spread_grad(attended_b, back_att_b)
+    term_out = weight_term(attended_b, back_att_b)
     sum_outb = jnp.sum(back_att, axis=(0, 1))
     back_attended = jnp.einsum(
         "rd,cd->rc", back_att_b, mat_out, preferred_element_type=jnp.float32
@@ -226,10 +318,10 @@
     value_terms = jnp.einsum(
         "shqk,sqhd->skhd", probs_b, back_attended, preferred_element_type=jnp.float32
     ).reshape(slot_total, -1, model_width)
-    back_keys, back_values = (
-        lax.psum_scatter(key_terms, "seq", scatter_dimension=1, tiled=True),
-        lax.psum_scatter(value_terms, "seq", scatter_dimension=1, tiled=True),
-    )
+    pair_terms = jnp.concatenate([key_terms, value_terms], axis=2)
+    pair_terms = pair_terms.reshape(slot_total, -1, tok_dev, 2 * model_width)
+    back_pairs = scatter_tree(jnp.moveaxis(pair_terms, 1, 0), ("seq",), jnp.bfloat16)
+    back_keys, back_values = back_pairs[:, :, :model_width], back_pairs[:, :, model_width:]
     back_qkv = jnp.concatenate(
         [
             back_queries.reshape(row_count, model_width),
@@ -239,8 +331,8 @@
         axis=1,
     )
     back_qkv_b = back_qkv.astype(jnp.bfloat16)
-    mat_qkv = collect_again(qkv_weight)
-    grad_qkvw = spread_grad(attn_in, back_qkv_b)
+    term_qkv = weight_term(attn_in, back_qkv_b)
+    grad_qkvw, grad_outw, grad_upw = spread_terms([term_qkv, term_out, term_up])
     sum_qkvb = jnp.sum(back_qkv, axis=0)
     back_attn_in = jnp.einsum(
         "rd,cd->rc", back_qkv_b, mat_qkv, preferred_element_type=jnp.float32
@@ -262,15 +354,22 @@
         axis=1,
     )
     modgrad_table = jnp.dot(slot_matches.T, slot_modgrad, precision=lax.Precision.HIGHEST)
-    modgrad_cols = lax.psum_scatter(modgrad_table, ("dp", "seq"), scatter_dimension=1, tiled=True)
+    modgrad_cols = scatter_tree(
+        jnp.moveaxis(modgrad_table.reshape(latent_count, -1, ada_bias.shape[0]), 1, 0),
+        ("dp", "seq"),
+    )
     grad_adaw = jnp.dot(
         rounded(jax.nn.silu(condition)).T, modgrad_cols, precision=lax.Precision.HIGHEST
     )
     grad_adab = jnp.sum(modgrad_cols, axis=0)
     cond_term = jnp.dot(modgrad_cols, rounded(ada_weight).T, precision=lax.Precision.HIGHEST)
-    cond_sum, total_qkvb, total_outb, total_upb, total_downb = lax.psum(
-        (cond_term, sum_qkvb, sum_outb, sum_upb, sum_downb), ("dp", "seq")
-    )
+    cond_sum = sum_tree(cond_term, ("dp", "seq"))
+    bias_sums = (sum_qkvb, sum_outb, sum_upb, sum_downb)
+    totals, start, bias_totals = sum_tree(jnp.concatenate(bias_sums), ("dp", "seq")), 0, []
+    for item in bias_sums:
+        bias_totals.append(totals[start : start + item.shape[0]])
+        start += item.shape[0]
+    total_qkvb, total_outb, total_upb, total_downb = bias_totals
     condition_grad = cond_sum * silu_slope(condition)
     seq_index = lax.axis_index("seq")
 

time: 1490 us -> 622 us (0.42)
  waiting for transfers between devices: 1190 us -> 431 us
  blocking collectives: 132 us -> 0 us
  starting transfers between devices: 1.13 us -> 26.9 us
  matrix products: 92 us -> 74.2 us
  other arithmetic: 27.4 us -> 44.1 us
    unnamed x22 -> x4, waiting for transfers between devices: 418 us -> 0.07 us
    reduce_scatter x5 -> x2, waiting for transfers between devices: 485 us -> 214 us  [spread_terms(): rows = lax.psum_scatter(joined, 'dp', scatter_dimension=0, tiled=True)]
    psum x1 -> x0, waiting for transfers between devices: 126 us -> none  [on_device(): lax.psum((cond_term, sum_qkvb, sum_outb, sum_upb, sum_downb), ('dp', 'seq'))]
    all_gather x8 -> x0, blocking collectives: 125 us -> none  [the longest x1 70 us: on_device(): modulation = lax.all_gather(mod_cols, ('dp', 'seq'), axis=1, tiled=True)]
    ppermute x0 -> x27, waiting for transfers between devices: none -> 90.7 us  [swap_bit(): return lax.ppermute(values, axes, [(i, i ^ step) for i in range(total)])]
    all_gather x4 -> x2, waiting for transfers between devices: 158 us -> 127 us  [the longest x1 73 us: on_device(): wide_full = lax.all_gather(wide_rows, 'dp', axis=0, tiled=True)]
    ppermute x0 -> x27, starting transfers between devices: none -> 26 us  [swap_bit(): return lax.ppermute(values, axes, [(i, i ^ step) for i in range(total)])]
    unnamed x199 -> x177, local copies, waits for them, and re-layouts: 25.2 us -> 4.8 us
  transfers between devices with their start and end apart: 16 -> 31, of which waited for: 14 -> 25; matrix products, arithmetic and copies ran while one was open for 5% -> 20% of each run, Pallas kernels for 0% -> 0%
where the time goes in v1:
time: 622 us; the launch traced here: 618 us
  waiting for transfers between devices  431 us (69%)
  matrix products  74.2 us (12%)
  other arithmetic  44.1 us (7%)
  starting transfers between devices  26.9 us (4%)
  local copies, waits for them, and re-layouts  24.3 us (4%)
  between operations  17 us (3%)
    reduce_scatter x2, waiting for transfers between devices, spread_terms(): rows = lax.psum_scatter(joined, 'dp', scatter_dimension=0, tiled=True)  214 us
    ppermute x27, waiting for transfers between devices, swap_bit(): return lax.ppermute(values, axes, [(i, i ^ step) for i in range(total)])  90.7 us
    all_gather x1, waiting for transfers between devices, on_device(): wide_full = lax.all_gather(wide_rows, 'dp', axis=0, tiled=True)  73 us
    all_gather x1, waiting for transfers between devices, on_device(): mat_down = lax.all_gather(down_rows, 'dp', axis=0, tiled=True)  53.9 us
    ppermute x27, starting transfers between devices, swap_bit(): return lax.ppermute(values, axes, [(i, i ^ step) for i in range(total)])  26 us
    dot_general x4, matrix products, weight_term(): jnp.einsum('rc,rd->cd', left, right, preferred_element_type=jnp.float32)  14.8 us
    concatenate x1, other arithmetic, spread_terms(): joined = jnp.concatenate(terms, axis=1) if len(terms) > 1 else terms[0]  14 us
  transfers between devices with their start and end apart: 31, of which 25 were waited for; matrix products, arithmetic and copies ran while one was open for 20% of the time, Pallas kernels for 0%

profile of v1, /device:TPU:0, one launch (start us, length us, event | category | flops | bytes accessed | tf_op | source)
XLA Modules:
  0.0 617.8 jit_solution(595256007388709948)
XLA Ops:
  11.0 3.0 collective-permute-start.5
  14.0 14.9 %collective-permute-done.5 = bf16[1,72,4608]{2,1,0:T(8,128)(2,1)S(1)} collective-permute-done((bf16[1,72,4608]{2,1,0:T(8,128)(2,1)S(1)}, bf16[1,72,4608]{2,1,0:T(8,128)(2,1)S(1)}, u32[]{:S(2)}, u32[]{:S(2)}) %collective-permute-start.5) | collective-permute-done | bytes 663584 | tf_op jit(solution)/shard_map/ppermute | solution.py:78
  31.8 1.8 collective-permute-start.8
  33.6 8.0 %collective-permute-done.8 = bf16[1,288,576]{2,1,0:T(8,128)(2,1)S(1)} collective-permute-done((bf16[1,288,576]{2,1,0:T(8,128)(2,1)S(1)}, bf16[1,288,576]{2,1,0:T(8,128)(2,1)S(1)}, u32[]{:S(2)}, u32[]{:S(2)}) %collective-permute-start.8) | collective-permute-done | bytes 331808 | tf_op jit(solution)/shard_map/ppermute | solution.py:78
  45.9 1.5 collective-permute-start
  50.8 1.6 collective-permute-start.2
  52.6 3.0 collective-permute-done.2
  57.8 3.9 collective-permute-done.3
  61.7 2.3 collective-permute-start.4
  64.2 9.6 %collective-permute-done.4 = f32[16,8,216]{2,1,0:T(8,128)S(1)} collective-permute-done((f32[16,8,216]{2,1,0:T(8,128)S(1)}, f32[16,8,216]{2,1,0:T(8,128)S(1)}, u32[]{:S(2)}, u32[]{:S(2)}) %collective-permute-start.4) | collective-permute-done | bytes 110624 | tf_op jit(solution)/shard_map/ppermute | solution.py:78
  74.5 73.0 %all-gather.3.cloned.1.call-done = bf16[1152,9216]{1,0:T(8,128)(2,1)} async-done(((bf16[72,9216]{1,0:T(8,128)(2,1)}), bf16[1152,9216]{1,0:T(8,128)(2,1)}) %all-gather.3.cloned.1.call-update) | async-done | bytes 21233680 | tf_op jit(solution)/shard_map/all_gather | solution.py:230
  147.5 4.8 fusion.15
  152.4 1.5 collective-permute-start.7
  154.5 13.5 %collective-permute-done.7 = bf16[1,1,128,2304]{3,2,1,0:T(8,128)(2,1)S(1)} collective-permute-done((bf16[1,1,128,2304]{3,2,1,0:T(8,128)(2,1)S(1)}, bf16[1,1,128,2304]{3,2,1,0:T(8,128)(2,1)S(1)}, u32[]{:S(2)}, u32[]{:S(2)}) %collective-permute-start.7) | collective-permute-done | bytes 589856 | tf_op jit(solution)/shard_map/ppermute | solution.py:78
  168.9 2.0 fusion.113
  170.9 2.0 fusion.33
  174.2 3.3 fusion.109
  177.8 7.5 %multiply_convert_fusion = (bf16[128,4608]{1,0:T(8,128)(2,1)S(1)}, f32[128,4608]{1,0:T(8,128)}) fusion(f32[4608]{0:T(1024)S(1)} %reshape.592, bf16[1152,9216]{1,0:T(8,128)(2,1)} %all-gather.3.cloned.1.call-done, f32[1,128,1152]{2,1,0:T(8,128)S(1)} %get-tuple-element.109, f32[1152]{0:T(1024)S(1)} %get-tuple-element.62, f32[1152]{0:T(1024)S(1)} %get-tuple-element.63, ...), kind=kOutput, calls=%fused_computation.31 | convolution fusion | flops 1365590016 | bytes 14774272 | tf_op jit(solution)/shard_map/dot_general | solution.py:278
  185.3 53.9 %all-gather.5.cloned.1.call-done = bf16[4608,1152]{1,0:T(8,128)(2,1)} async-done(((bf16[288,1152]{1,0:T(8,128)(2,1)}), bf16[4608,1152]{1,0:T(8,128)(2,1)}) %all-gather.5.cloned.1.call-update) | async-done | bytes 10616848 | tf_op jit(solution)/shard_map/all_gather | solution.py:237
  239.2 5.6 convolution_convert_fusion
  245.1 9.4 %fusion.114 = (f32[4608]{0:T(1024)}, bf16[128,4608]{1,0:T(8,128)(2,1)S(1)}) fusion(f32[128,4608]{1,0:T(8,128)} %get-tuple-element.147, bf16[4608,1152]{1,0:T(8,128)(2,1)} %all-gather.5.cloned.1.call-done, f32[1,128,1152]{2,1,0:T(8,128)} %param.39, f32[1152]{0:T(1024)S(1)} %get-tuple-element.61, pred[]{:T(512)} %bitcast.2), kind=kOutput, calls=%fused_computation.259 | convolution fusion | flops 1371188736 | bytes 14768641 | tf_op jit(solution)/shard_map/rd,fd->rf/dot_general | solution.py:289
  254.5 9.8 %fusion.39 = (f32[1152]{0:T(1024)}, f32[128]{0:T(128)S(1)}, f32[128,1152]{1,0:T(8,128)S(1)}) fusion(f32[1,128,1152]{2,1,0:T(8,128)S(1)} %get-tuple-element.109, f32[128]{0:T(128)S(1)} %add_rsqrt_fusion, f32[128]{0:T(128)S(1)} %broadcast_multiply_fusion.4, f32[1152]{0:T(1024)S(1)} %get-tuple-element.63, bf16[1152,9216]{1,0:T(8,128)(2,1)} %all-gather.3.cloned.1.call-done, ...), kind=kOutput, calls=%fused_computation.88 | convolution fusion | flops 1359985408 | bytes 12986880 | tf_op jit(solution)/shard_map/rf,cf->rc/dot_general | solution.py:295
  265.1 3.6 multiply_reduce_fusion.4
  269.5 2.7 convolution_convert_fusion.4
  273.2 1.5 fusion.117
  278.5 2.5 convolution_convert_fusion.3
  282.3 5.2 copy.98
  287.5 4.4 convolution_convert_fusion.1
  295.3 2.4 convolution_convert_fusion.2
  297.7 14.0 %pad_maximum_fusion = bf16[1152,9216]{1,0:T(8,128)(2,1)} fusion(bf16[1152,4608]{1,0:T(8,128)(2,1)S(1)} %convolution_convert_fusion.1, bf16[1152,1152]{1,0:T(8,128)(2,1)S(1)} %copy-done.1, bf16[1152,3456]{1,0:T(8,128)(2,1)S(1)} %convolution_convert_fusion.2), kind=kLoop, calls=%fused_computation.1 | loop fusion | flops 63700992 | bytes 42467328 | tf_op jit(solution)/shard_map/concatenate | solution.py:147
  312.2 6.6 %fusion.41 = (f32[1152]{0:T(1024)S(1)}, f32[128]{0:T(128)}, f32[128,1152]{1,0:T(8,128)S(1)}) fusion(f32[1,128,1152]{2,1,0:T(8,128)S(1)} %copy-done, f32[128]{0:T(128)S(1)} %copy-done.72, f32[128]{0:T(128)S(1)} %copy-done.65, f32[1152]{0:T(1024)S(1)} %get-tuple-element.65, bf16[1152,9216]{1,0:T(8,128)(2,1)} %all-gather.3.cloned.1.call-done, ...), kind=kOutput, calls=%fused_computation.92 | convolution fusion | flops 1022900992 | bytes 10922496 | tf_op jit(solution)/shard_map/rd,cd->rc/dot_general | solution.py:337
  323.9 1.7 collective-permute-start.10
  328.8 3.4 collective-permute-done.10
  333.1 2.1 collective-permute-start.24
  335.1 1.4 collective-permute-done.11
  341.8 4.2 collective-permute-done.25
  347.6 2.2 collective-permute-done.14
  350.9 3.2 collective-permute-done.15
  355.5 3.2 divide_subtract_fusion
  360.1 4.5 collective-permute-done.18
  366.2 2.3 reshape.594
  370.5 212.5 %reduce-scatter.3.cloned.1.call-done = bf16[72,9216]{1,0:T(8,128)(2,1)} async-done(((bf16[1152,9216]{1,0:T(8,128)(2,1)}), bf16[72,9216]{1,0:T(8,128)(2,1)}) %reduce-scatter.3.cloned.1.call-update) | async-done | bytes 1327120 | tf_op jit(solution)/shard_map/reduce_scatter | solution.py:148
  586.7 2.1 concatenate.111
  589.3 1.5 collective-permute-start.20
  591.5 2.8 divide_subtract_fusion.1
  594.3 11.6 %collective-permute-done.20 = bf16[1,72,4608]{2,1,0:T(8,128)(2,1)S(1)} collective-permute-done((bf16[1,72,4608]{2,1,0:T(8,128)(2,1)S(1)}, bf16[1,72,4608]{2,1,0:T(8,128)(2,1)S(1)}, u32[]{:S(2)}, u32[]{:S(2)}) %collective-permute-start.20) | collective-permute-done | bytes 663584 | tf_op jit(solution)/shard_map/ppermute | solution.py:78
  607.1 1.4 divide_subtract_fusion.3
  609.4 1.6 divide_subtract_fusion.2
  (356 shorter events, 60.3 us)
Async XLA Ops:
  7.2 140.3 %all-gather.3.cloned.1.call-start = ((), (), s32[]{:S(2)}) async-start(), calls=%async_computation.2 | async-start | bytes 22560768 | tf_op jit(solution)/shard_map/all_gather | solution.py:230
  11.0 17.9 %collective-permute-start.5 = (bf16[1,72,4608]{2,1,0:T(8,128)(2,1)S(1)}, bf16[1,72,4608]{2,1,0:T(8,128)(2,1)S(1)}, u32[]{:S(2)}, u32[]{:S(2)}) collective-permute-start(bf16[1,72,4608]{2,1,0:T(8,128)(2,1)S(1)} %concatenate.95), channel_id=1, source_target_pairs={{0,1},{1,0},{2,3},{3,2},{4,5},{5,4},{6,7},{7,6},{8,9},{9,8},{10,11... | collective-permute-start | bytes 1990664 | tf_op jit(solution)/shard_map/ppermute | solution.py:78
  31.7 207.5 %all-gather.5.cloned.1.call-start = ((), (), s32[]{:S(2)}) async-start(), calls=%async_computation.3 | async-start | bytes 11280384 | tf_op jit(solution)/shard_map/all_gather | solution.py:237
  31.8 9.8 %collective-permute-start.8 = (bf16[1,288,576]{2,1,0:T(8,128)(2,1)S(1)}, bf16[1,288,576]{2,1,0:T(8,128)(2,1)S(1)}, u32[]{:S(2)}, u32[]{:S(2)}) collective-permute-start(bf16[1,288,576]{2,1,0:T(8,128)(2,1)S(1)} %convert_bitcast_fusion), channel_id=1, source_target_pairs={{0,1},{1,0},{2,3},{3,2},{4,5},{5,4},{6,7},{7,6},{8,9},{9,8},{10,11... | collective-permute-start | bytes 995336 | tf_op jit(solution)/shard_map/ppermute | solution.py:78
  43.8 322.4 %reduce-scatter.5.cloned.1.call-start = ((), (), s32[]{:S(2)}) async-start(), calls=%async_computation.5 | async-start | bytes 11280384 | tf_op jit(solution)/shard_map/reduce_scatter | solution.py:148
  45.9 3.7 collective-permute-start
  47.6 16.4 %collective-permute-start.6 = (bf16[1,1,5184]{2,1,0:T(2,128)(2,1)S(1)}, bf16[1,1,5184]{2,1,0:T(2,128)(2,1)S(1)}, u32[]{:S(2)}, u32[]{:S(2)}) collective-permute-start(bf16[1,1,5184]{2,1,0:T(2,128)(2,1)S(1)} %concatenate.102), channel_id=1, source_target_pairs={{0,1},{1,0},{2,3},{3,2},{4,5},{5,4},{6,7},{7,6},{8,9},{9,8},{10,11... | collective-permute-start | bytes 31112 | tf_op jit(solution)/shard_map/ppermute | solution.py:78
  49.6 1.2 collective-permute-start.1
  49.7 97.9 %copy-start.64 = (f32[128]{0:T(128)}, f32[128]{0:T(128)S(1)}, u32[]{:S(2)}) copy-start(f32[128]{0:T(128)S(1)} %broadcast_multiply_fusion.5) | copy-start | bytes 1540
  50.8 4.8 collective-permute-start.2
  55.7 6.0 collective-permute-start.3
  56.5 91.1 %copy-start.71 = (f32[128]{0:T(128)}, f32[128]{0:T(128)S(1)}, u32[]{:S(2)}) copy-start(f32[128]{0:T(128)S(1)} %add_rsqrt_fusion.1) | copy-start | bytes 1540
  61.7 12.1 %collective-permute-start.4 = (f32[16,8,216]{2,1,0:T(8,128)S(1)}, f32[16,8,216]{2,1,0:T(8,128)S(1)}, u32[]{:S(2)}, u32[]{:S(2)}) collective-permute-start(f32[16,8,216]{2,1,0:T(8,128)S(1)} %pad_maximum_fusion.6), channel_id=1, source_target_pairs={{0,16},{1,17},{2,18},{3,19},{4,20},{5,21},{6,22},{7,23},{8,24},{9,... | collective-permute-start | bytes 331784 | tf_op jit(solution)/shard_map/ppermute | solution.py:78
  74.5 73.1 %copy-start.46 = (f32[1152]{0:T(1024)}, f32[1152]{0:T(1024)S(1)}, u32[]{:S(2)}) copy-start(f32[1152]{0:T(1024)S(1)} %get-tuple-element.64) | copy-start | bytes 13828
  74.5 103.3 %copy-start.49 = (f32[1152]{0:T(1024)}, f32[1152]{0:T(1024)S(1)}, u32[]{:S(2)}) copy-start(f32[1152]{0:T(1024)S(1)} %get-tuple-element.62) | copy-start | bytes 13828
  74.5 194.2 %copy-start.44 = (f32[1152]{0:T(1024)}, f32[1152]{0:T(1024)S(1)}, u32[]{:S(2)}) copy-start(f32[1152]{0:T(1024)S(1)} %get-tuple-element.66) | copy-start | bytes 13828
  152.4 15.5 %collective-permute-start.7 = (bf16[1,1,128,2304]{3,2,1,0:T(8,128)(2,1)S(1)}, bf16[1,1,128,2304]{3,2,1,0:T(8,128)(2,1)S(1)}, u32[]{:S(2)}, u32[]{:S(2)}) collective-permute-start(bf16[1,1,128,2304]{3,2,1,0:T(8,128)(2,1)S(1)} %maximum_bitcast_fusion.1), channel_id=1, source_target_pairs={{0,1},{1,0},{2,3},{3,2},{4,5},{5,4},{6,7},{7,6},{8,9},{9,8},{10,11... | collective-permute-start | bytes 1769480 | tf_op jit(solution)/shard_map/ppermute | solution.py:78
  177.6 87.5 %copy-start.63 = (f32[128]{0:T(128)}, f32[128]{0:T(128)S(1)}, u32[]{:S(2)}) copy-start(f32[128]{0:T(128)S(1)} %broadcast_multiply_fusion.4) | copy-start | bytes 1540
  177.8 87.3 %copy-start.70 = (f32[128]{0:T(128)}, f32[128]{0:T(128)S(1)}, u32[]{:S(2)}) copy-start(f32[128]{0:T(128)S(1)} %add_rsqrt_fusion) | copy-start | bytes 1540
  244.8 338.2 %reduce-scatter.3.cloned.1.call-start = ((), (), s32[]{:S(2)}) async-start(), calls=%async_computation.4 | async-start | bytes 22560768 | tf_op jit(solution)/shard_map/reduce_scatter | solution.py:148
  245.1 20.0 %slice-start = ((s8[10616832]{0:T(1024)(128)(4,1)}), s8[4194304]{0:T(1024)(128)(4,1)S(1)}, s32[]{:S(2)}) async-start(s8[10616832]{0:T(1024)(128)(4,1)} %bitcast.214), calls=%async_computation.6 | async-start | bytes 8388608
  245.1 20.0 %slice-start.1 = ((s8[10616832]{0:T(1024)(128)(4,1)}), s8[2228224]{0:T(1024)(128)(4,1)S(1)}, s32[]{:S(2)}) async-start(s8[10616832]{0:T(1024)(128)(4,1)} %bitcast.214), calls=%async_computation.7 | async-start | bytes 4456448
  277.3 15.7 %collective-permute-start.9 = (bf16[1,1,128,2304]{2,3,1,0:T(8,128)(2,1)}, bf16[1,1,128,2304]{2,3,1,0:T(8,128)(2,1)}, u32[]{:S(2)}, u32[]{:S(2)}) collective-permute-start(bf16[1,1,128,2304]{2,3,1,0:T(8,128)(2,1)} %fusion.37), channel_id=1, source_target_pairs={{0,1},{1,0},{2,3},{3,2},{4,5},{5,4},{6,7},{7,6},{8,9},{9,8},{10,11... | collective-permute-start | bytes 1769480 | tf_op jit(solution)/shard_map/ppermute | solution.py:78
  320.4 20.3 %copy-start.7 = (f32[1,128,1152]{2,1,0:T(8,128)S(1)}, f32[1,128,1152]{2,1,0:T(8,128)}, u32[]{:S(2)}) copy-start(f32[1,128,1152]{2,1,0:T(8,128)} %copy-done.5) | copy-start | bytes 1769476
  320.9 19.8 %copy-start.66 = (f32[128]{0:T(128)S(1)}, f32[128]{0:T(128)}, u32[]{:S(2)}) copy-start(f32[128]{0:T(128)} %copy-done.64) | copy-start | bytes 1540
  320.9 19.8 %copy-start.73 = (f32[128]{0:T(128)S(1)}, f32[128]{0:T(128)}, u32[]{:S(2)}) copy-start(f32[128]{0:T(128)} %copy-done.71) | copy-start | bytes 1540
  321.7 4.1 collective-permute-start.21
  323.9 8.3 %collective-permute-start.10 = (f32[16,8,216]{2,1,0:T(8,128)S(1)}, f32[16,8,216]{2,1,0:T(8,128)S(1)}, u32[]{:S(2)}, u32[]{:S(2)}) collective-permute-start(f32[16,8,216]{2,1,0:T(8,128)S(1)} %slice_select_fusion), channel_id=1, source_target_pairs={{0,16},{1,17},{2,18},{3,19},{4,20},{5,21},{6,22},{7,23},{8,24},{9,... | collective-permute-start | bytes 331784 | tf_op jit(solution)/shard_map/ppermute | solution.py:78
  326.6 1.3 collective-permute-start.22
  327.9 19.0 %copy-start.51 = (f32[2304]{0:T(1024)S(1)}, f32[2304]{0:T(1024)}, u32[]{:S(2)}) copy-start(f32[2304]{0:T(1024)} %param.47) | copy-start | bytes 27652
  327.9 21.9 %copy-start.12 = (bf16[1152,216]{0,1:T(8,128)(2,1)S(1)}, bf16[1152,216]{0,1:T(8,128)(2,1)}, u32[]{:S(2)}) copy-start(bf16[1152,216]{0,1:T(8,128)(2,1)} %copy-done.11) | copy-start | bytes 1492996
  327.9 5.0 collective-permute-start.23
  332.2 4.3 collective-permute-start.11
  333.0 21.2 %copy-start.60 = (f32[576]{0:T(1024)S(1)}, f32[576]{0:T(1024)}, u32[]{:S(2)}) copy-start(f32[576]{0:T(1024)} %param.45) | copy-start | bytes 6916
  333.0 21.2 %copy-start.77 = (f32[576]{0:T(1024)S(1)}, f32[576]{0:T(1024)}, u32[]{:S(2)}) copy-start(f32[576]{0:T(1024)} %param.55) | copy-start | bytes 6916
  333.0 21.2 %copy-start.78 = (f32[576]{0:T(1024)S(1)}, f32[576]{0:T(1024)}, u32[]{:S(2)}) copy-start(f32[576]{0:T(1024)} %param.65) | copy-start | bytes 6916
  333.1 5.2 collective-permute-start.24
  336.6 4.0 collective-permute-start.12
  338.3 7.7 %collective-permute-start.25 = (f32[10368]{0:T(1024)S(1)}, f32[10368]{0:T(1024)S(1)}, u32[]{:S(2)}, u32[]{:S(2)}) collective-permute-start(f32[10368]{0:T(1024)S(1)} %add.393), channel_id=1, source_target_pairs={{0,16},{1,17},{2,18},{3,19},{4,20},{5,21},{6,22},{7,23},{8,24},{9,... | collective-permute-start | bytes 124424 | tf_op jit(solution)/shard_map/ppermute | solution.py:78
  340.6 5.4 collective-permute-start.13
  346.1 3.7 collective-permute-start.14
  350.2 4.0 collective-permute-start.15
  354.2 1.2 collective-permute-start.16
  355.4 4.0 collective-permute-start.17
  359.4 5.1 collective-permute-start.18
  364.6 226.2 %collective-permute-start.19 = (f32[8,1152]{1,0:T(8,128)S(1)}, f32[8,1152]{1,0:T(8,128)S(1)}, u32[]{:S(2)}, u32[]{:S(2)}) collective-permute-start(f32[8,1152]{1,0:T(8,128)S(1)} %add.386), channel_id=1, source_target_pairs={{0,16},{1,17},{2,18},{3,19},{4,20},{5,21},{6,22},{7,23},{8,24},{9,... | collective-permute-start | bytes 110600 | tf_op jit(solution)/shard_map/ppermute | solution.py:78
  369.5 221.9 %collective-permute-start.26 = (bf16[1,288,576]{2,1,0:T(8,128)(2,1)}, bf16[1,288,576]{2,1,0:T(8,128)(2,1)}, u32[]{:S(2)}, u32[]{:S(2)}) collective-permute-start(bf16[1,288,576]{2,1,0:T(8,128)(2,1)} %select_convert_fusion.2), channel_id=1, source_target_pairs={{0,1},{1,0},{2,3},{3,2},{4,5},{5,4},{6,7},{7,6},{8,9},{9,8},{10,11... | collective-permute-start | bytes 995336 | tf_op jit(solution)/shard_map/ppermute | solution.py:78
  589.3 16.7 %collective-permute-start.20 = (bf16[1,72,4608]{2,1,0:T(8,128)(2,1)S(1)}, bf16[1,72,4608]{2,1,0:T(8,128)(2,1)S(1)}, u32[]{:S(2)}, u32[]{:S(2)}) collective-permute-start(bf16[1,72,4608]{2,1,0:T(8,128)(2,1)S(1)} %select_convert_fusion), channel_id=1, source_target_pairs={{0,1},{1,0},{2,3},{3,2},{4,5},{5,4},{6,7},{7,6},{8,9},{9,8},{10,11... | collective-permute-start | bytes 1990664 | tf_op jit(solution)/shard_map/ppermute | solution.py:78
  (71 other events, 497.9 us)
Sparse Core Ops, SparseCore 0:
  31.8 115.7 all-gather.2
  150.4 88.7 all-gather.4
  244.9 121.2 reduce-scatter.4
  370.2 212.7 reduce-scatter.2
